TPU v7x, 32 devices: a whole 2x2x4 slice. The times are simulated.
32 devices in a mesh: clus: 16 (over z, y, x), sub: 2 (over core).
Axes of the slice: x: 2, y: 2, z: 4, core: 2. Of those that a mesh axis runs over, the one named last changes fastest.
Arguments:
- dual_ops: float32 [64, 1536, 1536], P(('clus', 'sub')), may hold values from 0 to 3, as said below
- rigid_modes: float32 [64, 6, 1536], P(('clus', 'sub')), may hold values from -6 to 6
- members: int32 [64, 4, 1536], P(('clus', 'sub')), may hold values from 0 to 6144, as said below
- coarse_inverse: float32 [384, 384], P(('clus', 'sub')), may hold values from -1 to 1
- dual_rhs: float32 [64, 1536, 128], P(('clus', 'sub')), may hold values from -12 to 12
- coarse_rhs: float32 [64, 6, 128], P(('clus', 'sub')), may hold values from -512 to 512
Outputs:
- multipliers: float32 [64, 1536, 128], P(('clus', 'sub'))
- projected: float32 [64, 1536, 128], P(('clus', 'sub'))
Inputs may be any that keep to these rules, and one draw needn't show every extreme that they name: Every slot's group lists the slot itself first (its own position (s % 2) * 1536 + i), holds 1 to 4 slots of different subdomains, and is the same set for every slot in it; the group of every slot i >= 256 is that slot and one slot >= 256 of the other subdomain of the same device (members[s, 2:, i] = EMPTY); exported entries name only slots among the first 256 of a subdomain on devices with o in 0, 1, 2 that exist. Number the exported slots of a device k = 256 j + i for slot i of its j-th subdomain, and let E = 512: those with k < E / 4 are named only by groups of the other device of the same cluster; E / 4 <= k < E / 2 only by the device of cluster c + 1 with the same t; E / 2 <= k < 3 E / 4 only by the device of cluster c - 1 with the same t; 3 E / 4 <= k < 7 E / 8 only by the other device of the same cluster and the devices of cluster c + 1; 7 E / 8 <= k only by the other device of the same cluster and the devices of cluster c - 1. In each dual_ops[s] every row's off-diagonal entries sum in magnitude to less than its diagonal entry.
All inputs are finite; a program needn't handle non-finite values.
Results may differ from a plain program's by a relative error of at most 0.00015.
Values sent between devices are 32-bit elements; how exact they have to be, the bound alone decides.
A program may use at most 128 MiB of HBM per device.

v0:
```python
import jax
import jax.numpy as jnp
from jax import lax
from jax.sharding import PartitionSpec as P

ESUB = 256
ITERS = 2


def shifted(value, axis, steps):
    count = lax.axis_size(axis)
    leading, last = (max(0, -steps), min(count, count - steps))
    return lax.ppermute(value, axis, [(source, source + steps) for source in range(leading, last)])


def pair_product(first_field, second_field):
    return jnp.sum(first_field * second_field, axis=(0, 1))


def square_sum(field):
    return lax.psum(pair_product(field, field), ("clus", "sub"))


def on_device(dual_ops, rigid_modes, members, coarse_inverse, dual_rhs, coarse_rhs):
    sub_count, slot_count, load_cases = dual_rhs.shape
    local_rows = sub_count * slot_count
    export_rows = sub_count * ESUB
    pad_index = local_rows + 6 * export_rows
    quarter = export_rows // 4
    eighth = export_rows // 8
    share_rows = quarter + 4 * eighth
    group_count = members.shape[1]
    tables = jnp.transpose(members, (1, 0, 2)).reshape(group_count, local_rows)
    group_size = jnp.sum((tables < pad_index).astype(jnp.float32), axis=0)[:, None]
    offset = tables - local_rows
    cycle_block = offset // export_rows
    within = offset % export_rows
    inside = (tables >= local_rows) & (tables < pad_index)
    own_half = lax.axis_index("sub")
    neighbour = cycle_block // 2
    source_half = cycle_block % 2
    from_own = source_half == own_half
    above_start = local_rows + quarter + eighth
    pair_start = above_start + quarter + eighth
    shared_base = pair_start + source_half * share_rows
    lower_rows = jnp.where(
        within < 2 * quarter,
        local_rows + within - quarter,
        jnp.where(
            from_own,
            local_rows + quarter + within - 3 * quarter,
            shared_base + quarter + 2 * eighth + within - 3 * quarter,
        ),
    )
    upper_rows = jnp.where(
        within < 3 * quarter,
        above_start + within - 2 * quarter,
        jnp.where(
            from_own,
            above_start + quarter + within - 3 * quarter - eighth,
            shared_base + quarter + 3 * eighth + within - 3 * quarter - eighth,
        ),
    )
    pair_rows = jnp.where(
        within < quarter, shared_base + within, shared_base + quarter + within - 3 * quarter
    )
    remote = jnp.where(neighbour == 0, lower_rows, jnp.where(neighbour == 1, pair_rows, upper_rows))
    empty_at = pair_start + 2 * share_rows
    tables = jnp.where(tables < local_rows, tables, jnp.where(inside, remote, empty_at))
    other_members = tables[1:].reshape(-1)
    empty_row = jnp.zeros((1, load_cases), jnp.float32)

    def jump_part(field):
        flat_field = field.reshape(local_rows, load_cases)
        outgoing = field[:, :ESUB, :].reshape(export_rows, load_cases)
        upward = jnp.concatenate(
            [outgoing[quarter : 2 * quarter], outgoing[3 * quarter : 3 * quarter + eighth]], axis=0
        )
        downward = jnp.concatenate(
            [outgoing[2 * quarter : 3 * quarter], outgoing[3 * quarter + eighth :]], axis=0
        )
        below = shifted(upward, "clus", 1)
        above = shifted(downward, "clus", -1)
        shared = jnp.concatenate(
            [outgoing[:quarter], outgoing[3 * quarter :], below[quarter:], above[quarter:]], axis=0
        )
        gathered = jnp.concatenate(
            [below, above, lax.all_gather(shared, "sub", axis=0, tiled=True)], axis=0
        )
        pool_rows = jnp.concatenate([flat_field, gathered, empty_row], axis=0)
        picked = jnp.take(pool_rows, other_members, axis=0).reshape(
            group_count - 1, local_rows, load_cases
        )
        group_total = flat_field
        for member in range(group_count - 1):
            group_total = group_total + picked[member]
        return (flat_field - group_total / group_size).reshape(field.shape)

    def lift(terms):
        weights = jnp.dot(
            coarse_inverse,
            lax.all_gather(terms, ("clus", "sub"), axis=0, tiled=True),
            precision=lax.Precision.HIGHEST,
            preferred_element_type=jnp.float32,
        )
        weights = weights.reshape(sub_count, rigid_modes.shape[1], load_cases)
        return jump_part(
            jnp.einsum("jkm,jkn->jmn", rigid_modes, weights, precision=lax.Precision.HIGHEST)
        )

    def restrict(field):
        return jnp.einsum(
            "jkm,jmn->jkn", rigid_modes, field, precision=lax.Precision.HIGHEST
        ).reshape(-1, load_cases)

    def project(field):
        return field - lift(restrict(field))

    def blockwise(field):
        return jnp.einsum("jmq,jqn->jmn", dual_ops, field, precision=lax.Precision.HIGHEST)

    multipliers = lift(coarse_rhs.reshape(-1, load_cases))
    residual_now = jump_part(dual_rhs - blockwise(multipliers))
    projected = project(residual_now)
    direction = projected
    norm_now = square_sum(projected)
    for iteration in range(ITERS):
        along = jump_part(blockwise(direction))
        curvature_now = lax.psum(pair_product(direction, along), ("clus", "sub"))
        step_size = (norm_now / curvature_now)[None, None, :]
        multipliers = multipliers + step_size * direction
        residual_now = residual_now - step_size * along
        projected = project(residual_now)
        if iteration + 1 < ITERS:
            norm_next = square_sum(projected)
            direction = projected + (norm_next / norm_now)[None, None, :] * direction
            norm_now = norm_next
    return (multipliers, projected)


def solution(mesh):
    return jax.shard_map(
        on_device,
        mesh=mesh,
        in_specs=(
            P(("clus", "sub"), None, None),
            P(("clus", "sub"), None, None),
            P(("clus", "sub"), None, None),
            P(("clus", "sub"), None),
            P(("clus", "sub"), None, None),
            P(("clus", "sub"), None, None),
        ),
        out_specs=(P(("clus", "sub"), None, None), P(("clus", "sub"), None, None)),
        check_vma=False,
    )
```

profile of v0, /device:TPU:0, one launch (start us, length us, event | category | flops | bytes accessed | tf_op | source)
XLA Modules:
  0.0 818.4 jit_solution(16906384568805584855)
XLA Ops:
  1.4 43.9 %all-gather = f32[32,12,128]{2,1,0:T(8,128)S(1)} all-gather(f32[1,12,128]{2,1,0:T(8,128)S(1)} %reshape.286), channel_id=1, replica_groups=mesh['clus'=16,'sub'=2] {'clus','sub'}, dimensions={0}, use_global_device_ids=true | all-gather | bytes 202752 | tf_op jit(solution)/shard_map/all_gather | solution.py:102
  54.3 3.0 copy.77
  59.8 30.9 %gather_fusion = f32[9216,128]{1,0:T(8,128)} fusion(f32[4225,128]{1,0:T(8,128)S(1)} %dynamic-update-slice.34, s32[9216]{0:T(1024)S(1)} %fusion.17), kind=kCustom, calls=%fused_computation.clone | custom fusion | bytes 9474048 | tf_op jit(solution)/shard_map/jit(_take)/gather | solution.py:91
  90.8 6.6 broadcast_select_fusion.6
  98.9 3.1 copy.74
  105.2 3.2 divide_subtract_fusion.3
  108.4 23.3 %fusion = f32[2,1536,128]{1,2,0:T(8,128)S(1)} fusion(f32[2,1536,128]{1,2,0:T(8,128)S(1)} %copy-done.24, f32[2,1536,128]{1,2,0:T(8,128)S(1)} %divide_subtract_fusion.3, f32[2,1536,1536]{2,1,0:T(8,128)} %param.8), kind=kOutput, calls=%fused_computation.14 | convolution fusion | flops 7248150528 | bytes 23592960 | tf_op jit(solution)/shard_map/jmq,jqn->jmn/dot_general | solution.py:120
  133.5 4.6 collective-permute-start.2
  140.9 3.7 collective-permute-done.3
  147.0 30.9 %gather_fusion.1 = f32[9216,128]{1,0:T(8,128)} fusion(f32[4225,128]{1,0:T(8,128)S(1)} %dynamic-update-slice.29, s32[9216]{0:T(1024)S(1)} %fusion.17), kind=kCustom, calls=%fused_computation.1.clone | custom fusion | bytes 9474048 | tf_op jit(solution)/shard_map/jit(_take)/gather | solution.py:91
  178.0 6.6 broadcast_select_fusion.5
  186.1 3.0 copy.80
  192.4 3.0 divide_subtract_fusion.2
  198.0 38.8 %all-gather.1 = f32[32,12,128]{2,1,0:T(8,128)S(1)} all-gather(f32[1,12,128]{2,1,0:T(8,128)S(1)} %reshape.288), channel_id=1, replica_groups=mesh['clus'=16,'sub'=2] {'clus','sub'}, dimensions={0}, use_global_device_ids=true | all-gather | bytes 202752 | tf_op jit(solution)/shard_map/all_gather | solution.py:102
  240.4 2.2 collective-permute-start.4
  251.7 30.9 %gather_fusion.2 = f32[9216,128]{1,0:T(8,128)} fusion(f32[4225,128]{1,0:T(8,128)S(1)} %dynamic-update-slice.24, s32[9216]{0:T(1024)S(1)} %fusion.17), kind=kCustom, calls=%fused_computation.2.clone | custom fusion | bytes 9474048 | tf_op jit(solution)/shard_map/jit(_take)/gather | solution.py:91
  282.7 6.6 broadcast_select_fusion.4
  294.1 3.2 copy.89
  297.3 3.3 subtract_subtract_fusion.2
  300.6 23.3 %convolution_bitcast_fusion.3 = f32[2,1536,128]{1,2,0:T(8,128)S(1)} fusion(f32[2,1536,128]{1,2,0:T(8,128)S(1)} %subtract_subtract_fusion.2, f32[2,1536,1536]{2,1,0:T(8,128)} %param.8), kind=kOutput, calls=%fused_computation.10 | convolution fusion | flops 7247757312 | bytes 22020096 | tf_op jit(solution)/shard_map/jmq,jqn->jmn/dot_general | solution.py:120
  325.8 3.1 collective-permute-start.6
  338.1 30.9 %gather_fusion.3 = f32[9216,128]{1,0:T(8,128)} fusion(f32[4225,128]{1,0:T(8,128)S(1)} %dynamic-update-slice.19, s32[9216]{0:T(1024)S(1)} %fusion.17), kind=kCustom, calls=%fused_computation.3.clone | custom fusion | bytes 9474048 | tf_op jit(solution)/shard_map/jit(_take)/gather | solution.py:91
  369.0 6.6 broadcast_select_fusion.3
  377.1 3.1 copy.93
  383.5 4.7 multiply_reduce_fusion.2
  388.1 37.2 %all-reduce = (f32[128]{0:T(128)S(1)}, f32[128]{0:T(128)S(1)}) all-reduce(f32[128]{0:T(128)S(1)} %get-tuple-element.10, f32[128]{0:T(128)S(1)} %get-tuple-element.9), channel_id=1, replica_groups=mesh['clus'=16,'sub'=2] {'clus','sub'}, use_global_device_ids=true, to_apply=%region_2.4 | all-reduce | flops 256 | bytes 2048 | tf_op jit(solution)/shard_map/psum | solution.py:21
  429.7 41.2 %all-gather.2 = f32[32,12,128]{2,1,0:T(8,128)S(1)} all-gather(f32[1,12,128]{2,1,0:T(8,128)S(1)} %reshape.290), channel_id=1, replica_groups=mesh['clus'=16,'sub'=2] {'clus','sub'}, dimensions={0}, use_global_device_ids=true | all-gather | bytes 202752 | tf_op jit(solution)/shard_map/all_gather | solution.py:102
  478.6 2.1 collective-permute-done.8
  485.0 30.9 %gather_fusion.4 = f32[9216,128]{1,0:T(8,128)} fusion(f32[4225,128]{1,0:T(8,128)S(1)} %dynamic-update-slice.14, s32[9216]{0:T(1024)S(1)} %fusion.17), kind=kCustom, calls=%fused_computation.4.clone | custom fusion | bytes 9474048 | tf_op jit(solution)/shard_map/jit(_take)/gather | solution.py:91
  515.9 6.6 broadcast_select_fusion.2
  524.0 3.1 copy.101
  530.3 4.8 multiply_reduce_fusion.1
  535.2 37.0 %psum.30 = f32[128]{0:T(128)S(1)} all-reduce(f32[128]{0:T(128)S(1)} %get-tuple-element.15), channel_id=1, replica_groups=mesh['clus'=16,'sub'=2] {'clus','sub'}, use_global_device_ids=true, to_apply=%region_6.8 | all-reduce | flops 128 | bytes 1024 | tf_op jit(solution)/shard_map/psum | solution.py:21
  572.2 22.5 %convolution_bitcast_fusion.1 = f32[2,1536,128]{1,2,0:T(8,128)S(1)} fusion(f32[2,1536,1536]{2,1,0:T(8,128)} %param.8, f32[2,1536,128]{1,2,0:T(8,128)} %get-tuple-element.16, f32[2,1536,128]{1,2,0:T(8,128)S(1)} %copy-done.3, f32[128]{0:T(128)S(1)} %div.94), kind=kOutput, calls=%fused_computation.8 | convolution fusion | flops 7248543744 | bytes 23593472 | tf_op jit(solution)/shard_map/jmq,jqn->jmn/dot_general | solution.py:120
  596.6 4.2 collective-permute-start.10
  603.6 3.7 collective-permute-done.11
  609.5 30.9 %gather_fusion.5 = f32[9216,128]{1,0:T(8,128)} fusion(f32[4225,128]{1,0:T(8,128)S(1)} %dynamic-update-slice.9, s32[9216]{0:T(1024)S(1)} %fusion.17), kind=kCustom, calls=%fused_computation.5.clone | custom fusion | bytes 9474048 | tf_op jit(solution)/shard_map/jit(_take)/gather | solution.py:91
  640.5 6.6 broadcast_select_fusion.1
  648.6 3.1 copy.106
  655.0 5.3 multiply_reduce_fusion
  660.3 41.6 %psum.31 = f32[128]{0:T(128)S(1)} all-reduce(f32[128]{0:T(128)S(1)} %get-tuple-element.13), channel_id=1, replica_groups=mesh['clus'=16,'sub'=2] {'clus','sub'}, use_global_device_ids=true, to_apply=%region_8.10 | all-reduce | flops 128 | bytes 1024 | tf_op jit(solution)/shard_map/psum | solution.py:129
  701.9 3.1 convolution_bitcast_fusion.8
  705.0 41.2 %all-gather.3 = f32[32,12,128]{2,1,0:T(8,128)S(1)} all-gather(f32[1,12,128]{2,1,0:T(8,128)S(1)} %reshape.292), channel_id=1, replica_groups=mesh['clus'=16,'sub'=2] {'clus','sub'}, dimensions={0}, use_global_device_ids=true | all-gather | bytes 202752 | tf_op jit(solution)/shard_map/all_gather | solution.py:102
  760.3 30.9 %gather_fusion.6 = f32[9216,128]{1,0:T(8,128)} fusion(f32[4225,128]{1,0:T(8,128)S(1)} %dynamic-update-slice.4, s32[9216]{0:T(1024)S(1)} %fusion.17), kind=kCustom, calls=%fused_computation.6.clone | custom fusion | bytes 9474048 | tf_op jit(solution)/shard_map/jit(_take)/gather | solution.py:91
  791.2 6.6 broadcast_select_fusion
  802.7 3.2 copy.115
  805.9 7.6 subtract_subtract_fusion
  813.5 3.1 copy.118
  (248 shorter events, 117.2 us)
Async XLA Ops:
  0.6 45.7 %copy-start = (f32[2,6,1536]{2,0,1:T(2,128)S(1)}, f32[2,6,1536]{2,0,1:T(2,128)}, u32[]{:S(2)}) copy-start(f32[2,6,1536]{2,0,1:T(2,128)} %param.9) | copy-start | bytes 221188
  46.3 4.3 copy-start.26
  47.8 3.4 copy-start.19
  48.0 9.4 %collective-permute-start = (f32[192,128]{1,0:T(8,128)S(1)}, f32[192,128]{1,0:T(8,128)S(1)}, u32[]{:S(2)}, u32[]{:S(2)}) collective-permute-start(f32[192,128]{1,0:T(8,128)S(1)} %pad_maximum_fusion.7), channel_id=1, source_target_pairs={{0,2},{2,4},{4,6},{6,8},{8,10},{10,12},{12,14},{14,16},{16,18},{18... | collective-permute-start | bytes 294920 | tf_op jit(solution)/shard_map/ppermute | solution.py:13
  49.3 8.1 collective-permute-start.1
  103.6 1.6 copy-start.20
  105.2 3.2 copy-start.24
  108.4 23.3 %copy-start.23 = (f32[2,1536,128]{1,2,0:T(8,128)}, f32[2,1536,128]{1,2,0:T(8,128)S(1)}, u32[]{:S(2)}) copy-start(f32[2,1536,128]{1,2,0:T(8,128)S(1)} %divide_subtract_fusion.3) | copy-start | bytes 4718596
  131.7 1.8 copy-start.17
  133.5 7.4 collective-permute-start.2
  138.1 6.5 collective-permute-start.3
  190.7 1.7 copy-start.18
  195.4 1.1 copy-start.10
  196.6 40.2 %copy-start.27 = (f32[12,384]{1,0:T(8,128)S(1)}, f32[12,384]{1,0:T(8,128)}, u32[]{:S(2)}) copy-start(f32[12,384]{1,0:T(8,128)} %param.11) | copy-start | bytes 55300
  238.5 1.9 copy-start.15
  240.4 6.8 collective-permute-start.4
  242.6 6.7 collective-permute-start.5
  294.1 3.2 copy-start.11
  294.1 3.2 copy-start.16
  300.5 23.3 %copy-start.1 = (f32[2,1536,128]{1,2,0:T(8,128)}, f32[2,1536,128]{1,2,0:T(8,128)S(1)}, u32[]{:S(2)}) copy-start(f32[2,1536,128]{1,2,0:T(8,128)S(1)} %subtract_subtract_fusion.2) | copy-start | bytes 4718596
  323.9 1.9 copy-start.22
  325.8 7.5 collective-permute-start.6
  328.9 6.5 collective-permute-start.7
  381.8 1.6 copy-start.2
  383.5 41.9 %copy-start.12 = (f32[2,1536,128]{1,2,0:T(8,128)S(1)}, f32[2,1536,128]{1,2,0:T(8,128)}, u32[]{:S(2)}) copy-start(f32[2,1536,128]{1,2,0:T(8,128)} %copy-done.10) | copy-start | bytes 4718596
  427.1 1.1 copy-start.6
  472.6 1.9 copy-start.13
  474.5 6.2 collective-permute-start.8
  475.8 6.9 collective-permute-start.9
  528.7 1.6 copy-start.7
  530.3 41.9 %copy-start.3 = (f32[2,1536,128]{1,2,0:T(8,128)S(1)}, f32[2,1536,128]{1,2,0:T(8,128)}, u32[]{:S(2)}) copy-start(f32[2,1536,128]{1,2,0:T(8,128)} %copy-done.1) | copy-start | bytes 4718596
  594.7 1.9 copy-start.14
  596.6 7.0 collective-permute-start.10
  600.8 6.5 collective-permute-start.11
  653.4 1.6 copy-start.4
  655.0 46.9 %copy-start.8 = (f32[2,1536,128]{1,2,0:T(8,128)S(1)}, f32[2,1536,128]{1,2,0:T(8,128)}, u32[]{:S(2)}) copy-start(f32[2,1536,128]{1,2,0:T(8,128)} %copy-done.6) | copy-start | bytes 4718596
  747.9 1.9 copy-start.21
  749.8 6.2 collective-permute-start.12
  751.1 6.9 collective-permute-start.13
  802.7 3.2 copy-start.5
  802.7 3.2 copy-start.9
  813.5 3.1 copy-start.25
where the time goes:
time: 824 us; the launch traced here: 818 us
  local copies, waits for them, and re-layouts  308 us (37%)
  blocking collectives  295 us (36%)
  matrix products  82.4 us (10%)
  other arithmetic  80.8 us (10%)
  starting transfers between devices  26.9 us (3%)
  waiting for transfers between devices  23.1 us (3%)
    gather x7, local copies, waits for them, and re-layouts, jump_part(): jnp.take(pool_rows, other_members, axis=0)  217 us
    all_gather x4, blocking collectives, lift(): lax.all_gather(terms, ('clus', 'sub'), axis=0, tiled=True)  165 us
    psum x2, blocking collectives, square_sum(): return lax.psum(pair_product(field, field), ('clus', 'sub'))  74.2 us
    dot_general x3, matrix products, blockwise(): jnp.einsum('jmq,jqn->jmn', dual_ops, field, precision=lax.Precision.HIGHEST)  69.1 us
    select_n x7, other arithmetic, jump_part(): jnp.take(pool_rows, other_members, axis=0)  46.4 us
    squeeze x21, local copies, waits for them, and re-layouts, jump_part(): group_total = group_total + picked[member]  44.6 us
    psum x1, blocking collectives, on_device(): curvature_now = lax.psum(pair_product(direction, along), ('clus', 'sub'))  41.6 us
    ppermute x14, starting transfers between devices, shifted(): lax.ppermute(value, axis, [(source, source + steps) for source in range(l...  26.9 us
  transfers between devices with their start and end apart: 14, of which 10 were waited for; matrix products, arithmetic and copies ran while one was open for 2% of the time, Pallas kernels for 0%

commit v1 on v0

--- a/solution.py
+++ b/solution.py
@@ -18,7 +18,7 @@
 
 
 def square_sum(field):
-    return lax.psum(pair_product(field, field), ("clus", "sub"))
+    return lax.psum(lax.psum(pair_product(field, field), "sub"), "clus")
 
 
 def on_device(dual_ops, rigid_modes, members, coarse_inverse, dual_rhs, coarse_rhs):

time: 824 us -> 863 us (1.047)
  blocking collectives: 295 us -> 333 us
    psum x1 -> x2, blocking collectives: 41.6 us -> 74 us  [on_device(): curvature_now = lax.psum(pair_product(direction, along), ('clus', 'sub'))]
    psum x2 -> x4, blocking collectives: 74.2 us -> 83.6 us  [square_sum(): return lax.psum(lax.psum(pair_product(field, field), 'sub'), 'clus')]
  transfers between devices with their start and end apart: 14 -> 14, of which waited for: 10 -> 11; matrix products, arithmetic and copies ran while one was open for 2% -> 2% of each run, Pallas kernels for 0% -> 0%
where the time goes in v1:
time: 863 us; the launch traced here: 858 us
  blocking collectives  333 us (39%)
  local copies, waits for them, and re-layouts  308 us (36%)
  matrix products  82.4 us (10%)
  other arithmetic  80.7 us (9%)
  starting transfers between devices  28.1 us (3%)
  waiting for transfers between devices  22.9 us (3%)
    gather x7, local copies, waits for them, and re-layouts, jump_part(): jnp.take(pool_rows, other_members, axis=0)  217 us
    all_gather x4, blocking collectives, lift(): lax.all_gather(terms, ('clus', 'sub'), axis=0, tiled=True)  161 us
    psum x4, blocking collectives, square_sum(): return lax.psum(lax.psum(pair_product(field, field), 'sub'), 'clus')  83.6 us
    psum x2, blocking collectives, on_device(): curvature_now = lax.psum(pair_product(direction, along), ('clus', 'sub'))  74 us
    dot_general x3, matrix products, blockwise(): jnp.einsum('jmq,jqn->jmn', dual_ops, field, precision=lax.Precision.HIGHEST)  69.1 us
    select_n x7, other arithmetic, jump_part(): jnp.take(pool_rows, other_members, axis=0)  46.4 us
    squeeze x21, local copies, waits for them, and re-layouts, jump_part(): group_total = group_total + picked[member]  44.5 us
    ppermute x14, starting transfers between devices, shifted(): lax.ppermute(value, axis, [(source, source + steps) for source in range(l...  28.1 us
  transfers between devices with their start and end apart: 14, of which 11 were waited for; matrix products, arithmetic and copies ran while one was open for 2% of the time, Pallas kernels for 0%

profile of v1, /device:TPU:0, one launch (start us, length us, event | category | flops | bytes accessed | tf_op | source)
XLA Modules:
  0.0 857.6 jit_solution(184340779485826565)
XLA Ops:
  1.4 43.9 %all-gather = f32[32,12,128]{2,1,0:T(8,128)S(1)} all-gather(f32[1,12,128]{2,1,0:T(8,128)S(1)} %reshape.286), channel_id=1, replica_groups=mesh['clus'=16,'sub'=2] {'clus','sub'}, dimensions={0}, use_global_device_ids=true | all-gather | bytes 202752 | tf_op jit(solution)/shard_map/all_gather | solution.py:102
  54.3 3.0 copy.77
  59.8 31.0 %gather_fusion = f32[9216,128]{1,0:T(8,128)} fusion(f32[4225,128]{1,0:T(8,128)S(1)} %dynamic-update-slice.34, s32[9216]{0:T(1024)S(1)} %fusion.17), kind=kCustom, calls=%fused_computation.clone | custom fusion | bytes 9474048 | tf_op jit(solution)/shard_map/jit(_take)/gather | solution.py:91
  90.9 6.6 broadcast_select_fusion.6
  99.0 3.1 copy.74
  105.3 3.2 divide_subtract_fusion.3
  108.4 23.3 %fusion = f32[2,1536,128]{1,2,0:T(8,128)S(1)} fusion(f32[2,1536,128]{1,2,0:T(8,128)S(1)} %copy-done.24, f32[2,1536,128]{1,2,0:T(8,128)S(1)} %divide_subtract_fusion.3, f32[2,1536,1536]{2,1,0:T(8,128)} %param.8), kind=kOutput, calls=%fused_computation.14 | convolution fusion | flops 7248150528 | bytes 23592960 | tf_op jit(solution)/shard_map/jmq,jqn->jmn/dot_general | solution.py:120
  133.6 4.6 collective-permute-start.2
  141.0 3.7 collective-permute-done.3
  147.1 31.0 %gather_fusion.1 = f32[9216,128]{1,0:T(8,128)} fusion(f32[4225,128]{1,0:T(8,128)S(1)} %dynamic-update-slice.29, s32[9216]{0:T(1024)S(1)} %fusion.17), kind=kCustom, calls=%fused_computation.1.clone | custom fusion | bytes 9474048 | tf_op jit(solution)/shard_map/jit(_take)/gather | solution.py:91
  178.1 6.6 broadcast_select_fusion.5
  186.2 3.0 copy.80
  192.5 3.0 divide_subtract_fusion.2
  198.1 38.8 %all-gather.1 = f32[32,12,128]{2,1,0:T(8,128)S(1)} all-gather(f32[1,12,128]{2,1,0:T(8,128)S(1)} %reshape.288), channel_id=1, replica_groups=mesh['clus'=16,'sub'=2] {'clus','sub'}, dimensions={0}, use_global_device_ids=true | all-gather | bytes 202752 | tf_op jit(solution)/shard_map/all_gather | solution.py:102
  251.8 31.0 %gather_fusion.2 = f32[9216,128]{1,0:T(8,128)} fusion(f32[4225,128]{1,0:T(8,128)S(1)} %dynamic-update-slice.24, s32[9216]{0:T(1024)S(1)} %fusion.17), kind=kCustom, calls=%fused_computation.2.clone | custom fusion | bytes 9474048 | tf_op jit(solution)/shard_map/jit(_take)/gather | solution.py:91
  282.9 6.6 broadcast_select_fusion.4
  294.2 3.2 copy.89
  297.4 3.3 subtract_subtract_fusion.2
  300.7 23.3 %convolution_bitcast_fusion.3 = f32[2,1536,128]{1,2,0:T(8,128)S(1)} fusion(f32[2,1536,128]{1,2,0:T(8,128)S(1)} %subtract_subtract_fusion.2, f32[2,1536,1536]{2,1,0:T(8,128)} %param.8), kind=kOutput, calls=%fused_computation.10 | convolution fusion | flops 7247757312 | bytes 22020096 | tf_op jit(solution)/shard_map/jmq,jqn->jmn/dot_general | solution.py:120
  325.9 3.1 collective-permute-start.6
  338.2 31.0 %gather_fusion.3 = f32[9216,128]{1,0:T(8,128)} fusion(f32[4225,128]{1,0:T(8,128)S(1)} %dynamic-update-slice.19, s32[9216]{0:T(1024)S(1)} %fusion.17), kind=kCustom, calls=%fused_computation.3.clone | custom fusion | bytes 9474048 | tf_op jit(solution)/shard_map/jit(_take)/gather | solution.py:91
  369.3 6.6 broadcast_select_fusion.3
  377.3 3.1 copy.93
  383.7 4.7 multiply_reduce_fusion.2
  388.3 37.2 %psum.44 = f32[128]{0:T(128)S(1)} all-reduce(f32[128]{0:T(128)S(1)} %get-tuple-element.9), channel_id=1, replica_groups=mesh['clus'=16,'sub'=2] {'clus','sub'}, use_global_device_ids=true, to_apply=%region_5.7 | all-reduce | flops 128 | bytes 1024 | tf_op jit(solution)/shard_map/psum | solution.py:129
  428.0 40.8 %psum.43 = f32[128]{0:T(128)S(1)} all-reduce(f32[128]{0:T(128)S(1)} %psum.42), channel_id=1, replica_groups=mesh['clus'=16,'sub'=2] {'clus'}, use_global_device_ids=true, to_apply=%region_3.5 | all-reduce | flops 128 | bytes 1024 | tf_op jit(solution)/shard_map/psum | solution.py:21
  473.1 37.0 %all-gather.2 = f32[32,12,128]{2,1,0:T(8,128)S(1)} all-gather(f32[1,12,128]{2,1,0:T(8,128)S(1)} %reshape.290), channel_id=1, replica_groups=mesh['clus'=16,'sub'=2] {'clus','sub'}, dimensions={0}, use_global_device_ids=true | all-gather | bytes 202752 | tf_op jit(solution)/shard_map/all_gather | solution.py:102
  513.7 3.9 collective-permute-start.8
  526.5 31.0 %gather_fusion.4 = f32[9216,128]{1,0:T(8,128)} fusion(f32[4225,128]{1,0:T(8,128)S(1)} %dynamic-update-slice.14, s32[9216]{0:T(1024)S(1)} %fusion.17), kind=kCustom, calls=%fused_computation.4.clone | custom fusion | bytes 9474048 | tf_op jit(solution)/shard_map/jit(_take)/gather | solution.py:91
  557.5 6.6 broadcast_select_fusion.2
  565.6 3.1 copy.101
  571.9 4.8 multiply_reduce_fusion.1
  579.2 37.9 %psum.46 = f32[128]{0:T(128)S(1)} all-reduce(f32[128]{0:T(128)S(1)} %psum.45), channel_id=1, replica_groups=mesh['clus'=16,'sub'=2] {'clus'}, use_global_device_ids=true, to_apply=%region_8.10 | all-reduce | flops 128 | bytes 1024 | tf_op jit(solution)/shard_map/psum | solution.py:21
  617.1 22.5 %convolution_bitcast_fusion.1 = f32[2,1536,128]{1,2,0:T(8,128)S(1)} fusion(f32[2,1536,1536]{2,1,0:T(8,128)} %param.8, f32[2,1536,128]{1,2,0:T(8,128)} %get-tuple-element.14, f32[2,1536,128]{1,2,0:T(8,128)S(1)} %copy-done.3, f32[128]{0:T(128)S(1)} %div.94), kind=kOutput, calls=%fused_computation.8 | convolution fusion | flops 7248543744 | bytes 23593472 | tf_op jit(solution)/shard_map/jmq,jqn->jmn/dot_general | solution.py:120
  641.5 2.7 collective-permute-start.10
  647.4 3.4 collective-permute-done.11
  653.0 31.0 %gather_fusion.5 = f32[9216,128]{1,0:T(8,128)} fusion(f32[4225,128]{1,0:T(8,128)S(1)} %dynamic-update-slice.9, s32[9216]{0:T(1024)S(1)} %fusion.17), kind=kCustom, calls=%fused_computation.5.clone | custom fusion | bytes 9474048 | tf_op jit(solution)/shard_map/jit(_take)/gather | solution.py:91
  684.0 6.6 broadcast_select_fusion.1
  692.2 3.1 copy.106
  698.5 5.3 multiply_reduce_fusion
  703.8 36.8 %psum.47 = f32[128]{0:T(128)S(1)} all-reduce(f32[128]{0:T(128)S(1)} %get-tuple-element.11), channel_id=1, replica_groups=mesh['clus'=16,'sub'=2] {'clus','sub'}, use_global_device_ids=true, to_apply=%region_10.12 | all-reduce | flops 128 | bytes 1024 | tf_op jit(solution)/shard_map/psum | solution.py:129
  740.6 3.1 convolution_bitcast_fusion.8
  743.7 41.6 %all-gather.3 = f32[32,12,128]{2,1,0:T(8,128)S(1)} all-gather(f32[1,12,128]{2,1,0:T(8,128)S(1)} %reshape.292), channel_id=1, replica_groups=mesh['clus'=16,'sub'=2] {'clus','sub'}, dimensions={0}, use_global_device_ids=true | all-gather | bytes 202752 | tf_op jit(solution)/shard_map/all_gather | solution.py:102
  799.4 31.0 %gather_fusion.6 = f32[9216,128]{1,0:T(8,128)} fusion(f32[4225,128]{1,0:T(8,128)S(1)} %dynamic-update-slice.4, s32[9216]{0:T(1024)S(1)} %fusion.17), kind=kCustom, calls=%fused_computation.6.clone | custom fusion | bytes 9474048 | tf_op jit(solution)/shard_map/jit(_take)/gather | solution.py:91
  830.4 6.6 broadcast_select_fusion
  841.8 3.2 copy.115
  845.0 7.6 subtract_subtract_fusion
  852.6 3.1 copy.118
  (251 shorter events, 125.1 us)
Async XLA Ops:
  0.6 45.7 %copy-start = (f32[2,6,1536]{2,0,1:T(2,128)S(1)}, f32[2,6,1536]{2,0,1:T(2,128)}, u32[]{:S(2)}) copy-start(f32[2,6,1536]{2,0,1:T(2,128)} %param.9) | copy-start | bytes 221188
  46.3 4.3 copy-start.26
  47.8 3.4 copy-start.19
  48.0 9.4 %collective-permute-start = (f32[192,128]{1,0:T(8,128)S(1)}, f32[192,128]{1,0:T(8,128)S(1)}, u32[]{:S(2)}, u32[]{:S(2)}) collective-permute-start(f32[192,128]{1,0:T(8,128)S(1)} %pad_maximum_fusion.7), channel_id=1, source_target_pairs={{0,2},{2,4},{4,6},{6,8},{8,10},{10,12},{12,14},{14,16},{16,18},{18... | collective-permute-start | bytes 294920 | tf_op jit(solution)/shard_map/ppermute | solution.py:13
  49.3 8.1 collective-permute-start.1
  103.6 1.6 copy-start.20
  105.3 3.2 copy-start.24
  108.4 23.3 %copy-start.23 = (f32[2,1536,128]{1,2,0:T(8,128)}, f32[2,1536,128]{1,2,0:T(8,128)S(1)}, u32[]{:S(2)}) copy-start(f32[2,1536,128]{1,2,0:T(8,128)S(1)} %divide_subtract_fusion.3) | copy-start | bytes 4718596
  131.7 1.8 copy-start.17
  133.6 7.4 collective-permute-start.2
  138.1 6.5 collective-permute-start.3
  190.8 1.7 copy-start.18
  195.5 1.1 copy-start.10
  196.7 40.2 %copy-start.27 = (f32[12,384]{1,0:T(8,128)S(1)}, f32[12,384]{1,0:T(8,128)}, u32[]{:S(2)}) copy-start(f32[12,384]{1,0:T(8,128)} %param.11) | copy-start | bytes 55300
  238.6 1.9 copy-start.15
  240.5 6.8 collective-permute-start.4
  242.7 6.7 collective-permute-start.5
  294.2 3.2 copy-start.11
  294.2 3.2 copy-start.16
  300.7 23.3 %copy-start.1 = (f32[2,1536,128]{1,2,0:T(8,128)}, f32[2,1536,128]{1,2,0:T(8,128)S(1)}, u32[]{:S(2)}) copy-start(f32[2,1536,128]{1,2,0:T(8,128)S(1)} %subtract_subtract_fusion.2) | copy-start | bytes 4718596
  324.1 1.9 copy-start.22
  325.9 7.5 collective-permute-start.6
  329.1 6.5 collective-permute-start.7
  382.0 1.6 copy-start.2
  383.7 85.1 %copy-start.12 = (f32[2,1536,128]{1,2,0:T(8,128)S(1)}, f32[2,1536,128]{1,2,0:T(8,128)}, u32[]{:S(2)}) copy-start(f32[2,1536,128]{1,2,0:T(8,128)} %copy-done.10) | copy-start | bytes 4718596
  470.5 1.1 copy-start.6
  511.9 1.9 copy-start.13
  513.7 8.5 collective-permute-start.8
  517.7 6.7 collective-permute-start.9
  570.3 1.6 copy-start.7
  571.9 45.2 %copy-start.3 = (f32[2,1536,128]{1,2,0:T(8,128)S(1)}, f32[2,1536,128]{1,2,0:T(8,128)}, u32[]{:S(2)}) copy-start(f32[2,1536,128]{1,2,0:T(8,128)} %copy-done.1) | copy-start | bytes 4718596
  639.6 1.9 copy-start.14
  641.5 5.9 collective-permute-start.10
  644.3 6.5 collective-permute-start.11
  696.9 1.6 copy-start.4
  698.5 42.1 %copy-start.8 = (f32[2,1536,128]{1,2,0:T(8,128)S(1)}, f32[2,1536,128]{1,2,0:T(8,128)}, u32[]{:S(2)}) copy-start(f32[2,1536,128]{1,2,0:T(8,128)} %copy-done.6) | copy-start | bytes 4718596
  787.0 1.9 copy-start.21
  788.9 6.2 collective-permute-start.12
  790.2 6.9 collective-permute-start.13
  841.8 3.2 copy-start.5
  841.8 3.2 copy-start.9
  852.6 3.1 copy-start.25
